TPU v7x, 32 devices: a whole 2x2x4 slice. The times are simulated.
32 devices in a mesh: mem: 8 (over z, core), slab: 4 (over y, x).
Axes of the slice: x: 2, y: 2, z: 4, core: 2. Of those that a mesh axis runs over, the one named last changes fastest.
Arguments:
- thickness: float32 [64, 256, 384], P('mem', 'slab'), may hold values from 0.5 to 2.5
- face_u: float32 [256, 384], P('slab'), may hold values from -0.4 to 0.4
- face_v: float32 [256, 384], P('slab'), may hold values from -0.4 to 0.4
- obs_cells: int32 [512, 4], P('slab'), may hold values from 0 to 98303, as said below
- obs_weights: int32 [512, 4], P('slab'), may hold values from 1 to 4
- obs_values: float32 [512], P('slab'), may hold values from -6 to 6
- obs_noise: float32 [64, 512], P('mem', 'slab'), may hold values from -3 to 3
- cov_inverse: float32 [512, 512], P('slab'), may hold values from -0.375 to 0.375
- taper_mask: int32 [4, 4], replicated, may hold values from 0 to 1, as said below
Outputs:
- analysis: float32 [64, 256, 384], P('mem', 'slab')
Inputs may be any that keep to these rules, and one draw needn't show every extreme that they name: `obs_cells`: observation o covers a 2 x 2 square of cells, all within the rows of slab o // 128. `taper_mask`: entries are 0 or 1 and the diagonal is 1.
All inputs are finite; a program needn't handle non-finite values.
Results may differ from a plain program's by a relative error of at most 0.0003.
Values sent between devices are 32-bit elements; how exact they have to be, the bound alone decides.
A program may use at most 64 MiB of HBM per device.

v0:
```python
import jax
import jax.numpy as jnp
from jax import lax
from jax.sharding import PartitionSpec as P


def padded_2(block, sides, width):
    for axis, dim in sides:
        count = lax.axis_size(axis)
        forward = [(i, i + 1) for i in range(count - 1)]
        backward = [(target, source) for source, target in forward]
        low = lax.ppermute(
            lax.slice_in_dim(block, block.shape[dim] - width, None, axis=dim), axis, forward
        )
        high = lax.ppermute(lax.slice_in_dim(block, 0, width, axis=dim), axis, backward)
        block = jnp.concatenate([low, block, high], axis=dim)
    return block


def minmod(first_diff, second_diff):
    return (
        0.5
        * (jnp.sign(first_diff) + jnp.sign(second_diff))
        * jnp.minimum(jnp.abs(first_diff), jnp.abs(second_diff))
    )


def face_flux(padded, velocity, axis_dim):
    counted = padded.shape[axis_dim] - 3
    far_low = lax.slice_in_dim(padded, 0, counted, axis=axis_dim)
    near_low = lax.slice_in_dim(padded, 1, 1 + counted, axis=axis_dim)
    near_high = lax.slice_in_dim(padded, 2, 2 + counted, axis=axis_dim)
    far_high = lax.slice_in_dim(padded, 3, 3 + counted, axis=axis_dim)
    left_state = near_low + 0.5 * minmod(near_low - far_low, near_high - near_low)
    right_state = near_high - 0.5 * minmod(near_high - near_low, far_high - near_high)
    return jnp.maximum(velocity, 0.0) * left_state + jnp.minimum(velocity, 0.0) * right_state


def local(
    thickness,
    face_u,
    face_v,
    obs_cells,
    obs_weights,
    obs_values,
    obs_noise,
    cov_inverse,
    taper_mask,
):
    member_subset = thickness.shape[0]
    band_rows = thickness.shape[1]
    column_list = thickness.shape[2]
    slab_index = lax.axis_index("slab")
    stacked = jnp.concatenate([thickness, face_v[None]], 0)
    padded = padded_2(stacked, (("slab", 1),), 2)
    row_pad = padded[:member_subset]
    row_speed = padded[member_subset, 2 : band_rows + 3]
    row_fluxes = face_flux(row_pad, row_speed, 1)
    col_pad = jnp.pad(thickness, ((0, 0), (0, 0), (2, 2)))
    col_speed = jnp.pad(face_u, ((0, 0), (0, 1)))
    column_fluxes = face_flux(col_pad, col_speed, 2)
    prior_state = (
        thickness
        - (column_fluxes[:, :, 1:] - column_fluxes[:, :, :-1])
        - (row_fluxes[:, 1:, :] - row_fluxes[:, :-1, :])
    )
    state_vector = prior_state.reshape(member_subset, band_rows * column_list)
    local_cells = obs_cells - slab_index * (band_rows * column_list)
    weights = obs_weights.astype(jnp.float32)
    picked = state_vector[:, local_cells]
    obs_model = jnp.sum(picked * weights[None], -1) / jnp.sum(weights, -1)[None]
    innovation = obs_values[None, :] + obs_noise - obs_model
    white_terms = jnp.dot(innovation, cov_inverse, precision=lax.Precision.HIGHEST)
    whitened = lax.psum_scatter(white_terms, "slab", scatter_dimension=1, tiled=True)
    model_all, white_all = (
        lax.all_gather(obs_model, "mem", axis=0, tiled=True),
        lax.all_gather(whitened, "mem", axis=0, tiled=True),
    )
    obs_mean = jnp.mean(model_all, 0, keepdims=True)
    cell_state = lax.all_to_all(state_vector, "mem", split_axis=1, concat_axis=0, tiled=True)
    members = cell_state.shape[0]
    anomaly = cell_state - jnp.mean(cell_state, 0, keepdims=True)
    obs_anomaly = model_all - obs_mean
    anom_full, white_full = (
        lax.all_gather(obs_anomaly, "slab", axis=1, tiled=True),
        lax.all_gather(white_all, "slab", axis=1, tiled=True),
    )
    block_size = obs_anomaly.shape[1]
    mask_row = lax.dynamic_slice_in_dim(taper_mask, slab_index, 1, 0)[0].astype(jnp.float32)
    taper_row = jnp.repeat(mask_row, block_size)
    cross = lax.dot_general(
        anomaly, anom_full, (((0,), (0,)), ((), ())), precision=lax.Precision.HIGHEST
    ) / (members - 1)
    tapered = cross * taper_row[None, :]
    update = lax.dot_general(
        white_full, tapered, (((1,), (1,)), ((), ())), precision=lax.Precision.HIGHEST
    )
    analysis_cells = cell_state + update
    returned = lax.all_to_all(analysis_cells, "mem", split_axis=0, concat_axis=1, tiled=True)
    return returned.reshape(member_subset, band_rows, column_list)


def solution(mesh):
    return jax.shard_map(
        local,
        mesh=mesh,
        in_specs=(
            P("mem", "slab", None),
            P("slab", None),
            P("slab", None),
            P("slab", None),
            P("slab", None),
            P("slab"),
            P("mem", "slab"),
            P("slab", None),
            P(),
        ),
        out_specs=P("mem", "slab", None),
        check_vma=False,
    )
```

profile of v0, /device:TPU:0, one launch (start us, length us, event | category | flops | bytes accessed | tf_op | source)
XLA Modules:
  0.0 138.8 jit_solution(13175700690734752969)
XLA Ops:
  6.5 0.0 copy-start
  6.5 0.0 copy-start.1
  6.5 1.1 pad_maximum_fusion.3
  7.6 1.3 collective-permute-start
  8.9 5.5 %collective-permute-start.1 = (f32[9,2,384]{2,1,0:T(2,128)S(1)}, f32[9,2,384]{2,1,0:T(2,128)S(1)}, u32[]{:S(2)}, u32[]{:S(2)}) collective-permute-start(f32[9,2,384]{2,1,0:T(2,128)S(1)} %get-tuple-element.9), channel_id=1, source_target_pairs={{0,1},{1,2},{2,3},{4,5},{5,6},{6,7},{8,9},{9,10},{10,11},{12,13},{... | collective-permute-start | bytes 82952 | tf_op jit(solution)/shard_map/ppermute | solution.py:12
  14.4 0.9 pad_maximum_fusion.1
  15.4 0.7 compare_select_fusion
  16.1 0.1 copy.36
  16.2 0.1 reshape.37
  16.3 3.6 %multiply_add_fusion = f32[8,64,385]{2,1,0:T(8,128)S(1)} fusion(f32[8,64,384]{2,1,0:T(8,128)} %param.9, f32[64,385]{1,0:T(8,128)S(1)} %get-tuple-element.12, f32[64,385]{1,0:T(8,128)S(1)} %get-tuple-element.11), kind=kLoop, calls=%fused_computation.12 | loop fusion | flops 4730880 | bytes 1772032 | tf_op jit(solution)/shard_map/add | solution.py:36
  19.9 0.7 convert_reduce_fusion
  20.6 0.0 collective-permute-done
  20.6 0.9 maximum_bitcast_fusion
  21.6 0.0 collective-permute-done.1
  21.6 1.6 %maximum_maximum_fusion = (f32[9,66,384]{2,1,0:T(8,128)S(1)}, f32[9,66,384]{2,1,0:T(8,128)S(1)}) fusion(f32[1,64,384]{2,1,0:T(8,128)} %bitcast.30, f32[8,64,384]{2,1,0:T(8,128)} %param.9, f32[9,2,384]{2,1,0:T(2,128)S(1)} %collective-permute-done.1, f32[9,2,384]{2,1,0:T(2,128)S(1)} %collective-permute-done), kind=kLoop, calls=%fused_computation.14 | loop fusion | flops 912384 | bytes 2764800 | tf_op jit(solution)/shard_map/concatenate | solution.py:16
  23.2 0.0 copy-start.2
  23.2 1.3 multiply_add_fusion.1
  24.5 0.0 copy-done.1
  24.5 0.3 fusion.11
  24.9 0.1 all_to_all.26
  25.0 1.3 copy.34
  26.4 5.4 %all-to-all-start = ((f32[8,8,3072]{2,0,1:T(8,128)}), f32[8,8,3072]{2,0,1:T(8,128)S(1)}, u32[]{:S(2)}, u32[]{:S(2)}) async-start(f32[8,8,3072]{2,0,1:T(8,128)} %copy.34), calls=%async_computation | async-start | bytes 1572864 | tf_op jit(solution)/shard_map/all_to_all | solution.py:80
  31.8 0.0 reduce-scatter.2.cloned.1.call-start
  31.8 0.7 multiply_bitcast_fusion
  32.5 0.0 copy-done.2
  32.5 0.1 copy.37
  32.6 0.1 broadcast_bitcast_fusion
  32.7 0.0 copy-start.3
  32.7 6.6 %copy.35 = f32[8,64,384]{0,2,1:T(8,128)} copy(f32[8,64,384]{2,1,0:T(8,128)S(1)} %fusion.11) | data formatting | bytes 1572864 | tf_op jit(solution)/shard_map/sub | solution.py:63
  39.2 5.6 %gather_fusion = f32[512,8]{1,0:T(8,128)S(1)} fusion(f32[8,24576]{0,1:T(8,128)} %bitcast.25, s32[1024]{0:T(1024)S(1)} %pad_clamp_fusion), kind=kCustom, calls=%fused_computation | custom fusion | bytes 34816 | tf_op jit(solution)/shard_map/gather | solution.py:70
  44.9 0.2 multiply_reduce_fusion
  45.2 0.0 copy-done
  45.2 0.0 copy-done.3
  45.2 0.0 copy-done.4
  45.2 0.8 fusion.15
  46.0 0.0 reduce-scatter.2.cloned.1.call-update
  46.1 14.6 %all_gather.14 = f32[64,128]{1,0:T(8,128)S(1)} all-gather(f32[8,128]{1,0:T(8,128)S(1)} %divide_bitcast_fusion), channel_id=1, replica_groups=mesh['mem'=8,'slab'=4] {'mem'}, dimensions={0}, use_global_device_ids=true | all-gather | bytes 36864 | tf_op jit(solution)/shard_map/all_gather | solution.py:76
  60.7 9.9 %all_gather.15 = f32[64,512]{1,0:T(8,128)S(1)} all-gather(f32[64,128]{1,0:T(8,128)S(1)} %broadcast_subtract_fusion), channel_id=1, replica_groups=mesh['mem'=8,'slab'=4] {'slab'}, dimensions={1}, use_global_device_ids=true | all-gather | bytes 163840 | tf_op jit(solution)/shard_map/all_gather | solution.py:85
  70.6 0.0 reduce-scatter.2.cloned.1.call-done
  70.6 14.2 %all_gather.12 = f32[64,128]{1,0:T(8,128)S(1)} all-gather(f32[8,128]{1,0:T(8,128)} %reduce-scatter.2.cloned.1.call-done), channel_id=1, replica_groups=mesh['mem'=8,'slab'=4] {'mem'}, dimensions={0}, use_global_device_ids=true | all-gather | bytes 36864 | tf_op jit(solution)/shard_map/all_gather | solution.py:77
  84.7 9.0 %all_gather.13 = f32[64,512]{1,0:T(8,128)S(1)} all-gather(f32[64,128]{1,0:T(8,128)S(1)} %all_gather.12), channel_id=1, replica_groups=mesh['mem'=8,'slab'=4] {'slab'}, dimensions={1}, use_global_device_ids=true | all-gather | bytes 163840 | tf_op jit(solution)/shard_map/all_gather | solution.py:86
  93.8 0.0 all-to-all-done
  93.8 0.1 reduce_sum.38
  93.8 5.2 %fusion.13 = f32[3072,512]{1,0:T(8,128)S(1)} fusion(f32[64,512]{1,0:T(8,128)S(1)} %all_gather.15, f32[8,8,3072]{2,0,1:T(8,128)S(1)} %all-to-all-done, f32[3072]{0:T(1024)S(1)} %broadcast_multiply_fusion), kind=kOutput, calls=%fused_computation.23 | convolution fusion | flops 1208156160 | bytes 7221248 | tf_op jit(solution)/shard_map/dot_general | solution.py:91
  99.0 6.0 %fusion.5 = f32[8,8,3072]{2,1,0:T(8,128)S(1)} fusion(f32[64,512]{1,0:T(8,128)S(1)} %all_gather.13, f32[3072,512]{1,0:T(8,128)S(1)} %fusion.13, f32[512]{0:T(512)S(1)} %broadcast_bitcast_fusion, f32[8,8,3072]{2,0,1:T(8,128)S(1)} %all-to-all-done), kind=kOutput, calls=%fused_computation.4 | convolution fusion | flops 1209729024 | bytes 7997440 | tf_op jit(solution)/shard_map/dot_general | solution.py:95
  105.1 25.4 %all_to_all.35 = f32[8,8,3072]{2,1,0:T(8,128)S(1)} all-to-all(f32[8,8,3072]{2,1,0:T(8,128)S(1)} %fusion.5), channel_id=1, replica_groups=mesh['mem'=8,'slab'=4] {'mem'}, dimensions={0} | all-to-all | bytes 1572864 | tf_op jit(solution)/shard_map/all_to_all | solution.py:99
  130.5 0.5 copy.39
  130.9 1.0 reshape.34
  (10 shorter events, 0.1 us)
Async XLA Ops:
  6.5 38.6 %copy-start = (f32[128,512]{1,0:T(8,128)S(1)}, f32[128,512]{1,0:T(8,128)}, u32[]{:S(2)}) copy-start(f32[128,512]{1,0:T(8,128)} %param.16) | copy-start | bytes 786436
  6.5 18.0 %copy-start.1 = (f32[8,64,384]{2,1,0:T(8,128)S(1)}, f32[8,64,384]{2,1,0:T(8,128)}, u32[]{:S(2)}) copy-start(f32[8,64,384]{2,1,0:T(8,128)} %param.9) | copy-start | bytes 2359300
  7.6 13.0 %collective-permute-start = (f32[9,2,384]{2,1,0:T(2,128)S(1)}, f32[9,2,384]{2,1,0:T(2,128)S(1)}, u32[]{:S(2)}, u32[]{:S(2)}) collective-permute-start(f32[9,2,384]{2,1,0:T(2,128)S(1)} %get-tuple-element.10), channel_id=1, source_target_pairs={{1,0},{2,1},{3,2},{5,4},{6,5},{7,6},{9,8},{10,9},{11,10},{13,12},{... | collective-permute-start | bytes 82952 | tf_op jit(solution)/shard_map/ppermute | solution.py:15
  8.9 12.6 %collective-permute-start.1 = (f32[9,2,384]{2,1,0:T(2,128)S(1)}, f32[9,2,384]{2,1,0:T(2,128)S(1)}, u32[]{:S(2)}, u32[]{:S(2)}) collective-permute-start(f32[9,2,384]{2,1,0:T(2,128)S(1)} %get-tuple-element.9), channel_id=1, source_target_pairs={{0,1},{1,2},{2,3},{4,5},{5,6},{6,7},{8,9},{9,10},{10,11},{12,13},{... | collective-permute-start | bytes 82952 | tf_op jit(solution)/shard_map/ppermute | solution.py:12
  23.2 9.3 %copy-start.2 = (s32[128,4]{0,1:T(4,128)S(1)}, s32[128,4]{0,1:T(4,128)}, u32[]{:S(2)}) copy-start(s32[128,4]{0,1:T(4,128)} %param.13) | copy-start | bytes 6148
  26.4 67.4 %all-to-all-start = ((f32[8,8,3072]{2,0,1:T(8,128)}), f32[8,8,3072]{2,0,1:T(8,128)S(1)}, u32[]{:S(2)}, u32[]{:S(2)}) async-start(f32[8,8,3072]{2,0,1:T(8,128)} %copy.34), calls=%async_computation | async-start | bytes 1572864 | tf_op jit(solution)/shard_map/all_to_all | solution.py:80
  31.8 38.8 %reduce-scatter.2.cloned.1.call-start = ((), (), s32[]{:S(2)}) async-start(), calls=%async_computation.3 | async-start | bytes 20480 | tf_op jit(solution)/shard_map/reduce_scatter | solution.py:74
  32.7 12.5 %copy-start.3 = (f32[8,128]{1,0:T(8,128)S(1)}, f32[8,128]{1,0:T(8,128)}, u32[]{:S(2)}) copy-start(f32[8,128]{1,0:T(8,128)} %param.15) | copy-start | bytes 12292
  32.7 12.5 %copy-start.4 = (f32[128]{0:T(128)S(1)}, f32[128]{0:T(128)}, u32[]{:S(2)}) copy-start(f32[128]{0:T(128)} %param.14) | copy-start | bytes 1540
Sparse Core Ops, SparseCore 0:
  46.2 24.1 reduce-scatter.1
where the time goes:
time: 139 us
  blocking collectives  73 us (53%)
  local copies, waits for them, and re-layouts  15.6 us (11%)
  between operations  13.6 us (10%)
  other arithmetic  12.3 us (9%)
  starting transfers between devices  12.2 us (9%)
  matrix products  12.1 us (9%)
    all_to_all x1, blocking collectives, local(): lax.all_to_all(analysis_cells, 'mem', split_axis=0, concat_axis=1, tiled=...  25.4 us
    all_gather x1, blocking collectives, local(): lax.all_gather(obs_model, 'mem', axis=0, tiled=True)  14.6 us
    all_gather x1, blocking collectives, local(): lax.all_gather(whitened, 'mem', axis=0, tiled=True)  14.2 us
    all_gather x1, blocking collectives, local(): lax.all_gather(obs_anomaly, 'slab', axis=1, tiled=True)  9.86 us
    all_gather x1, blocking collectives, local(): lax.all_gather(white_all, 'slab', axis=1, tiled=True)  9 us
    sub x1, local copies, waits for them, and re-layouts, local(): thickness - (column_fluxes[:, :, 1:] - column_fluxes[:, :, :-1])  6.56 us
    dot_general x1, matrix products, local(): lax.dot_general(white_full, tapered, (((1,), (1,)), ((), ())), precision=...  6.04 us
    gather x1, local copies, waits for them, and re-layouts, local(): picked = state_vector[:, local_cells]  5.6 us
  transfers between devices with their start and end apart: 4, of which 0 were waited for; matrix products, arithmetic and copies ran while one was open for 15% of the time, Pallas kernels for 0%

commit v1 on v0

--- a/solution.py
+++ b/solution.py
@@ -2,6 +2,31 @@
 import jax.numpy as jnp
 from jax import lax
 from jax.sharding import PartitionSpec as P
+
+
+def cut_along(array, dim, peers):
+    shape = array.shape
+    pieces = array.reshape(*shape[:dim], peers, shape[dim] // peers, *shape[dim + 1 :])
+    return jnp.moveaxis(pieces, dim, 0)
+
+
+def in_order(blocks, dim):
+    blocks = jnp.moveaxis(blocks, 0, dim)
+    shape = blocks.shape
+    return blocks.reshape(*shape[:dim], shape[dim] * shape[dim + 1], *shape[dim + 2 :])
+
+
+def exchange_directly(value, axis, split_dim, concat_dim):
+    devices, index = (lax.axis_size(axis), lax.axis_index(axis))
+    blocks = cut_along(value, split_dim, devices)
+    gathered = [blocks[index]]
+    for step in range(1, devices):
+        sent = blocks[(index + step) % devices]
+        gathered.append(
+            lax.ppermute(sent, axis, [(i, (i + step) % devices) for i in range(devices)])
+        )
+    blocks = jnp.stack(gathered)[(index - jnp.arange(devices)) % devices]
+    return in_order(blocks, concat_dim)
 
 
 def padded_2(block, sides, width):
@@ -96,7 +121,7 @@
         white_full, tapered, (((1,), (1,)), ((), ())), precision=lax.Precision.HIGHEST
     )
     analysis_cells = cell_state + update
-    returned = lax.all_to_all(analysis_cells, "mem", split_axis=0, concat_axis=1, tiled=True)
+    returned = exchange_directly(analysis_cells, "mem", 0, 1)
     return returned.reshape(member_subset, band_rows, column_list)
 
 

time: 139 us -> 134 us (0.964)
  the two profiles are of different devices: /device:TPU:0 before, /device:TPU:9 now
where the time goes in v1:
time: 134 us
  blocking collectives  44.6 us (33%)
  starting transfers between devices  20.6 us (15%)
  local copies, waits for them, and re-layouts  16.3 us (12%)
  waiting for transfers between devices  13.9 us (10%)
  between operations  13.8 us (10%)
  other arithmetic  12.3 us (9%)
  matrix products  12.1 us (9%)
    all_gather x1, blocking collectives, local(): lax.all_gather(whitened, 'mem', axis=0, tiled=True)  15.4 us
    all_gather x1, blocking collectives, local(): lax.all_gather(obs_model, 'mem', axis=0, tiled=True)  14.3 us
    ppermute x7, waiting for transfers between devices, exchange_directly(): lax.ppermute(sent, axis, [(i, (i + step) % devices) for i in range(device...  13 us
    ppermute x7, starting transfers between devices, exchange_directly(): lax.ppermute(sent, axis, [(i, (i + step) % devices) for i in range(device...  9.17 us
    all_gather x1, blocking collectives, local(): lax.all_gather(obs_anomaly, 'slab', axis=1, tiled=True)  7.85 us
    all_gather x1, blocking collectives, local(): lax.all_gather(white_all, 'slab', axis=1, tiled=True)  7.06 us
    sub x1, local copies, waits for them, and re-layouts, local(): thickness - (column_fluxes[:, :, 1:] - column_fluxes[:, :, :-1])  6.59 us
    all_to_all x1, starting transfers between devices, local(): lax.all_to_all(state_vector, 'mem', split_axis=1, concat_axis=0, tiled=True)  6.16 us
  transfers between devices with their start and end apart: 11, of which 5 were waited for; matrix products, arithmetic and copies ran while one was open for 16% of the time, Pallas kernels for 0%

profile of v1, /device:TPU:9, one launch (start us, length us, event | category | flops | bytes accessed | tf_op | source)
XLA Modules:
  0.0 133.6 jit_solution(4389033448942409546)
XLA Ops:
  6.5 1.1 pad_maximum_fusion.3
  7.6 1.3 collective-permute-start
  8.9 4.0 %collective-permute-start.1 = (f32[9,2,384]{2,1,0:T(2,128)S(1)}, f32[9,2,384]{2,1,0:T(2,128)S(1)}, u32[]{:S(2)}, u32[]{:S(2)}) collective-permute-start(f32[9,2,384]{2,1,0:T(2,128)S(1)} %get-tuple-element.9), channel_id=1, source_target_pairs={{0,1},{1,2},{2,3},{4,5},{5,6},{6,7},{8,9},{9,10},{10,11},{12,13},{... | collective-permute-start | bytes 82952 | tf_op jit(solution)/shard_map/ppermute | solution.py:37
  12.9 0.9 pad_maximum_fusion.1
  13.9 0.7 compare_select_fusion
  14.5 0.1 copy.36
  14.7 0.1 reshape.82
  14.8 0.7 convert_reduce_fusion
  15.5 3.6 %multiply_add_fusion = f32[8,64,385]{2,1,0:T(8,128)S(1)} fusion(f32[8,64,384]{2,1,0:T(8,128)} %param.9, f32[64,385]{1,0:T(8,128)S(1)} %get-tuple-element.20, f32[64,385]{1,0:T(8,128)S(1)} %get-tuple-element.19), kind=kLoop, calls=%fused_computation.13 | loop fusion | flops 4730880 | bytes 1772032 | tf_op jit(solution)/shard_map/add | solution.py:61
  19.1 0.9 maximum_bitcast_fusion
  20.1 1.6 %maximum_maximum_fusion = (f32[9,66,384]{2,1,0:T(8,128)S(1)}, f32[9,66,384]{2,1,0:T(8,128)S(1)}) fusion(f32[1,64,384]{2,1,0:T(8,128)} %bitcast.60, f32[8,64,384]{2,1,0:T(8,128)} %param.9, f32[9,2,384]{2,1,0:T(2,128)S(1)} %collective-permute-done.1, f32[9,2,384]{2,1,0:T(2,128)S(1)} %collective-permute-done), kind=kLoop, calls=%fused_computation.15 | loop fusion | flops 912384 | bytes 2764800 | tf_op jit(solution)/shard_map/concatenate | solution.py:41
  21.7 1.3 multiply_add_fusion.1
  23.1 0.3 fusion.11
  23.4 0.1 all_to_all.14
  23.5 1.3 %copy.34 = f32[8,8,3072]{2,0,1:T(8,128)} copy(f32[8,8,3072]{2,1,0:T(8,128)S(1)} %all_to_all.14) | data formatting | bytes 1572864 | tf_op jit(solution)/shard_map/all_to_all | solution.py:105
  24.9 6.2 %all-to-all-start = ((f32[8,8,3072]{2,0,1:T(8,128)}), f32[8,8,3072]{2,0,1:T(8,128)S(1)}, u32[]{:S(2)}, u32[]{:S(2)}) async-start(f32[8,8,3072]{2,0,1:T(8,128)} %copy.34), calls=%async_computation | async-start | bytes 1572864 | tf_op jit(solution)/shard_map/all_to_all | solution.py:105
  31.0 0.7 fusion.22
  31.8 0.1 copy.37
  32.0 0.1 broadcast_bitcast_fusion
  32.0 6.6 %copy.35 = f32[8,64,384]{0,2,1:T(8,128)} copy(f32[8,64,384]{2,1,0:T(8,128)S(1)} %fusion.11) | data formatting | bytes 1572864 | tf_op jit(solution)/shard_map/sub | solution.py:88
  38.6 5.6 %gather_fusion = f32[512,8]{1,0:T(8,128)S(1)} fusion(f32[8,24576]{0,1:T(8,128)} %bitcast.55, s32[1024]{0:T(1024)S(1)} %pad_clamp_fusion.1), kind=kCustom, calls=%fused_computation | custom fusion | bytes 34816 | tf_op jit(solution)/shard_map/gather | solution.py:95
  44.2 0.2 multiply_reduce_fusion
  44.6 0.0 copy-done.3
  44.6 0.8 fusion.15
  45.4 0.0 reduce-scatter.2.cloned.1.call-update
  45.5 14.3 %all_gather.14 = f32[64,128]{1,0:T(8,128)S(1)} all-gather(f32[8,128]{1,0:T(8,128)S(1)} %divide_bitcast_fusion), channel_id=1, replica_groups=mesh['mem'=8,'slab'=4] {'mem'}, dimensions={0}, use_global_device_ids=true | all-gather | bytes 36864 | tf_op jit(solution)/shard_map/all_gather | solution.py:101
  59.8 7.9 %all_gather.15 = f32[64,512]{1,0:T(8,128)S(1)} all-gather(f32[64,128]{1,0:T(8,128)S(1)} %broadcast_subtract_fusion), channel_id=1, replica_groups=mesh['mem'=8,'slab'=4] {'slab'}, dimensions={1}, use_global_device_ids=true | all-gather | bytes 163840 | tf_op jit(solution)/shard_map/all_gather | solution.py:110
  67.6 0.9 reduce-scatter.2.cloned.1.call-done
  68.5 15.4 %all_gather.12 = f32[64,128]{1,0:T(8,128)S(1)} all-gather(f32[8,128]{1,0:T(8,128)} %reduce-scatter.2.cloned.1.call-done), channel_id=1, replica_groups=mesh['mem'=8,'slab'=4] {'mem'}, dimensions={0}, use_global_device_ids=true | all-gather | bytes 36864 | tf_op jit(solution)/shard_map/all_gather | solution.py:102
  83.9 7.1 %all_gather.13 = f32[64,512]{1,0:T(8,128)S(1)} all-gather(f32[64,128]{1,0:T(8,128)S(1)} %all_gather.12), channel_id=1, replica_groups=mesh['mem'=8,'slab'=4] {'slab'}, dimensions={1}, use_global_device_ids=true | all-gather | bytes 163840 | tf_op jit(solution)/shard_map/all_gather | solution.py:111
  91.0 0.1 reduce_sum.38
  91.0 5.2 %fusion.13 = f32[3072,512]{1,0:T(8,128)S(1)} fusion(f32[64,512]{1,0:T(8,128)S(1)} %all_gather.15, f32[8,8,3072]{2,0,1:T(8,128)S(1)} %all-to-all-done, f32[3072]{0:T(1024)S(1)} %broadcast_multiply_fusion), kind=kOutput, calls=%fused_computation.24 | convolution fusion | flops 1208156160 | bytes 7221248 | tf_op jit(solution)/shard_map/dot_general | solution.py:116
  96.2 6.0 %fusion.5 = f32[8,8,3072]{2,1,0:T(8,128)S(1)} fusion(f32[64,512]{1,0:T(8,128)S(1)} %all_gather.13, f32[3072,512]{1,0:T(8,128)S(1)} %fusion.13, f32[512]{0:T(512)S(1)} %broadcast_bitcast_fusion, f32[8,8,3072]{2,0,1:T(8,128)S(1)} %all-to-all-done), kind=kOutput, calls=%fused_computation.5 | convolution fusion | flops 1209729024 | bytes 7997440 | tf_op jit(solution)/shard_map/dot_general | solution.py:120
  102.3 0.1 dynamic-slice_bitcast_fusion
  102.3 1.5 %collective-permute-start.2 = (f32[8,3072]{1,0:T(8,128)S(1)}, f32[8,3072]{1,0:T(8,128)S(1)}, u32[]{:S(2)}, u32[]{:S(2)}) collective-permute-start(f32[8,3072]{1,0:T(8,128)S(1)} %get-tuple-element.17), channel_id=1, source_target_pairs={{0,4},{4,8},{8,12},{12,16},{16,20},{20,24},{24,28},{28,0},{1,5},{5... | collective-permute-start | bytes 294920 | tf_op jit(solution)/shard_map/ppermute | solution.py:26
  103.9 3.0 %collective-permute-start.3 = (f32[8,3072]{1,0:T(8,128)S(1)}, f32[8,3072]{1,0:T(8,128)S(1)}, u32[]{:S(2)}, u32[]{:S(2)}) collective-permute-start(f32[8,3072]{1,0:T(8,128)S(1)} %get-tuple-element.16), channel_id=1, source_target_pairs={{0,8},{4,12},{8,16},{12,20},{16,24},{20,28},{24,0},{28,4},{1,9},{5... | collective-permute-start | bytes 294920 | tf_op jit(solution)/shard_map/ppermute | solution.py:26
  106.9 0.3 collective-permute-start.4
  107.2 0.8 collective-permute-start.5
  108.0 2.0 %collective-permute-start.6 = (f32[8,3072]{1,0:T(8,128)S(1)}, f32[8,3072]{1,0:T(8,128)S(1)}, u32[]{:S(2)}, u32[]{:S(2)}) collective-permute-start(f32[8,3072]{1,0:T(8,128)S(1)} %get-tuple-element.13), channel_id=1, source_target_pairs={{0,20},{4,24},{8,28},{12,0},{16,4},{20,8},{24,12},{28,16},{1,21},{... | collective-permute-start | bytes 294920 | tf_op jit(solution)/shard_map/ppermute | solution.py:26
  110.1 1.2 collective-permute-start.7
  111.3 0.3 collective-permute-start.8
  111.6 0.7 collective-permute-done.4
  112.2 9.0 %collective-permute-done.5 = f32[8,3072]{1,0:T(8,128)S(1)} collective-permute-done((f32[8,3072]{1,0:T(8,128)S(1)}, f32[8,3072]{1,0:T(8,128)S(1)}, u32[]{:S(2)}, u32[]{:S(2)}) %collective-permute-start.5) | collective-permute-done | bytes 98336 | tf_op jit(solution)/shard_map/ppermute | solution.py:26
  121.3 3.3 %collective-permute-done.7 = f32[8,3072]{1,0:T(8,128)S(1)} collective-permute-done((f32[8,3072]{1,0:T(8,128)S(1)}, f32[8,3072]{1,0:T(8,128)S(1)}, u32[]{:S(2)}, u32[]{:S(2)}) %collective-permute-start.7) | collective-permute-done | bytes 98336 | tf_op jit(solution)/shard_map/ppermute | solution.py:26
  124.6 0.1 collective-permute-done.8
  124.7 0.6 gather_fusion.1
  125.3 0.5 copy.39
  125.7 1.0 reshape_reshape.3
  (34 shorter events, 0.2 us)
Async XLA Ops:
  6.5 38.0 %copy-start = (f32[128,512]{1,0:T(8,128)S(1)}, f32[128,512]{1,0:T(8,128)}, u32[]{:S(2)}) copy-start(f32[128,512]{1,0:T(8,128)} %param.16) | copy-start | bytes 786436
  6.5 16.5 %copy-start.1 = (f32[8,64,384]{2,1,0:T(8,128)S(1)}, f32[8,64,384]{2,1,0:T(8,128)}, u32[]{:S(2)}) copy-start(f32[8,64,384]{2,1,0:T(8,128)} %param.9) | copy-start | bytes 2359300
  7.6 11.5 %collective-permute-start = (f32[9,2,384]{2,1,0:T(2,128)S(1)}, f32[9,2,384]{2,1,0:T(2,128)S(1)}, u32[]{:S(2)}, u32[]{:S(2)}) collective-permute-start(f32[9,2,384]{2,1,0:T(2,128)S(1)} %get-tuple-element.10), channel_id=1, source_target_pairs={{1,0},{2,1},{3,2},{5,4},{6,5},{7,6},{9,8},{10,9},{11,10},{13,12},{... | collective-permute-start | bytes 82952 | tf_op jit(solution)/shard_map/ppermute | solution.py:40
  8.9 11.2 %collective-permute-start.1 = (f32[9,2,384]{2,1,0:T(2,128)S(1)}, f32[9,2,384]{2,1,0:T(2,128)S(1)}, u32[]{:S(2)}, u32[]{:S(2)}) collective-permute-start(f32[9,2,384]{2,1,0:T(2,128)S(1)} %get-tuple-element.9), channel_id=1, source_target_pairs={{0,1},{1,2},{2,3},{4,5},{5,6},{6,7},{8,9},{9,10},{10,11},{12,13},{... | collective-permute-start | bytes 82952 | tf_op jit(solution)/shard_map/ppermute | solution.py:37
  21.7 10.0 %copy-start.2 = (s32[128,4]{0,1:T(4,128)S(1)}, s32[128,4]{0,1:T(4,128)}, u32[]{:S(2)}) copy-start(s32[128,4]{0,1:T(4,128)} %param.13) | copy-start | bytes 6148
  24.9 66.1 %all-to-all-start = ((f32[8,8,3072]{2,0,1:T(8,128)}), f32[8,8,3072]{2,0,1:T(8,128)S(1)}, u32[]{:S(2)}, u32[]{:S(2)}) async-start(f32[8,8,3072]{2,0,1:T(8,128)} %copy.34), calls=%async_computation | async-start | bytes 1572864 | tf_op jit(solution)/shard_map/all_to_all | solution.py:105
  31.0 37.5 %reduce-scatter.2.cloned.1.call-start = ((), (), s32[]{:S(2)}) async-start(), calls=%async_computation.2 | async-start | bytes 20480 | tf_op jit(solution)/shard_map/reduce_scatter | solution.py:99
  32.0 12.5 %copy-start.3 = (f32[8,128]{1,0:T(8,128)S(1)}, f32[8,128]{1,0:T(8,128)}, u32[]{:S(2)}) copy-start(f32[8,128]{1,0:T(8,128)} %param.15) | copy-start | bytes 12292
  32.0 12.5 %copy-start.4 = (f32[128]{0:T(128)S(1)}, f32[128]{0:T(128)}, u32[]{:S(2)}) copy-start(f32[128]{0:T(128)} %param.14) | copy-start | bytes 1540
  102.3 7.7 %collective-permute-start.2 = (f32[8,3072]{1,0:T(8,128)S(1)}, f32[8,3072]{1,0:T(8,128)S(1)}, u32[]{:S(2)}, u32[]{:S(2)}) collective-permute-start(f32[8,3072]{1,0:T(8,128)S(1)} %get-tuple-element.17), channel_id=1, source_target_pairs={{0,4},{4,8},{8,12},{12,16},{16,20},{20,24},{24,28},{28,0},{1,5},{5... | collective-permute-start | bytes 294920 | tf_op jit(solution)/shard_map/ppermute | solution.py:26
  103.9 7.4 %collective-permute-start.3 = (f32[8,3072]{1,0:T(8,128)S(1)}, f32[8,3072]{1,0:T(8,128)S(1)}, u32[]{:S(2)}, u32[]{:S(2)}) collective-permute-start(f32[8,3072]{1,0:T(8,128)S(1)} %get-tuple-element.16), channel_id=1, source_target_pairs={{0,8},{4,12},{8,16},{12,20},{16,24},{20,28},{24,0},{28,4},{1,9},{5... | collective-permute-start | bytes 294920 | tf_op jit(solution)/shard_map/ppermute | solution.py:26
  106.9 5.4 %collective-permute-start.4 = (f32[8,3072]{1,0:T(8,128)S(1)}, f32[8,3072]{1,0:T(8,128)S(1)}, u32[]{:S(2)}, u32[]{:S(2)}) collective-permute-start(f32[8,3072]{1,0:T(8,128)S(1)} %get-tuple-element.15), channel_id=1, source_target_pairs={{0,12},{4,16},{8,20},{12,24},{16,28},{20,0},{24,4},{28,8},{1,13},{... | collective-permute-start | bytes 294920 | tf_op jit(solution)/shard_map/ppermute | solution.py:26
  107.2 14.1 %collective-permute-start.5 = (f32[8,3072]{1,0:T(8,128)S(1)}, f32[8,3072]{1,0:T(8,128)S(1)}, u32[]{:S(2)}, u32[]{:S(2)}) collective-permute-start(f32[8,3072]{1,0:T(8,128)S(1)} %get-tuple-element.14), channel_id=1, source_target_pairs={{0,16},{4,20},{8,24},{12,28},{16,0},{20,4},{24,8},{28,12},{1,17},{... | collective-permute-start | bytes 294920 | tf_op jit(solution)/shard_map/ppermute | solution.py:26
  108.0 13.2 %collective-permute-start.6 = (f32[8,3072]{1,0:T(8,128)S(1)}, f32[8,3072]{1,0:T(8,128)S(1)}, u32[]{:S(2)}, u32[]{:S(2)}) collective-permute-start(f32[8,3072]{1,0:T(8,128)S(1)} %get-tuple-element.13), channel_id=1, source_target_pairs={{0,20},{4,24},{8,28},{12,0},{16,4},{20,8},{24,12},{28,16},{1,21},{... | collective-permute-start | bytes 294920 | tf_op jit(solution)/shard_map/ppermute | solution.py:26
  110.1 14.5 %collective-permute-start.7 = (f32[8,3072]{1,0:T(8,128)S(1)}, f32[8,3072]{1,0:T(8,128)S(1)}, u32[]{:S(2)}, u32[]{:S(2)}) collective-permute-start(f32[8,3072]{1,0:T(8,128)S(1)} %get-tuple-element.12), channel_id=1, source_target_pairs={{0,24},{4,28},{8,0},{12,4},{16,8},{20,12},{24,16},{28,20},{1,25},{... | collective-permute-start | bytes 294920 | tf_op jit(solution)/shard_map/ppermute | solution.py:26
  111.3 13.4 %collective-permute-start.8 = (f32[8,3072]{1,0:T(8,128)S(1)}, f32[8,3072]{1,0:T(8,128)S(1)}, u32[]{:S(2)}, u32[]{:S(2)}) collective-permute-start(f32[8,3072]{1,0:T(8,128)S(1)} %get-tuple-element.11), channel_id=1, source_target_pairs={{0,28},{4,0},{8,4},{12,8},{16,12},{20,16},{24,20},{28,24},{1,29},{... | collective-permute-start | bytes 294920 | tf_op jit(solution)/shard_map/ppermute | solution.py:26
Sparse Core Ops, SparseCore 0:
  45.6 22.9 reduce-scatter.1
